TPU v7x, 128 devices: a whole 4x4x4 slice. The times are simulated.
128 devices in a mesh: dp: 64 (over y, z_hi, x, core), mod: 2 (over z_lo).
Axes of the slice: x: 4, y: 4, z: 4 (z_hi: 2, z_lo: 2; z = z_hi * 2 + z_lo), core: 2. Of those that a mesh axis runs over, the one named last changes fastest.
Arguments:
- tokens: bfloat16 [256, 256, 1024], P(('dp', 'mod')), may hold values from -6 to 6
- condition: bfloat16 [256, 1024], P(('dp', 'mod')), may hold values from -6 to 6
- occupied: int32 [256], P(('dp', 'mod')), may hold values from 0 to 1, as said below
- modulation_weight: bfloat16 [1024, 6144], P(None, 'mod'), may hold values from -0.1875 to 0.1875
- modulation_bias: float32 [6, 1024], P('mod'), may hold values from -3 to 3
- input_weight: bfloat16 [1024, 3072], replicated, may hold values from -0.1875 to 0.1875
- query_bias: float32 [1024], replicated, may hold values from -3 to 3
- value_bias: float32 [1024], replicated, may hold values from -3 to 3
- output_weight: bfloat16 [1024, 1024], replicated, may hold values from -1.5 to 1.5
- output_bias: float32 [1024], replicated, may hold values from -3 to 3
- expand_weight: bfloat16 [1024, 4096], replicated, may hold values from -0.1875 to 0.1875
- expand_bias: float32 [4096], replicated, may hold values from -3 to 3
- contract_weight: bfloat16 [4096, 1024], replicated, may hold values from -0.1875 to 0.1875
- contract_bias: float32 [1024], replicated, may hold values from -3 to 3
- cotangent: bfloat16 [256, 256, 1024], P(('dp', 'mod')), may hold values from -6 to 6
Outputs:
- layer_out: float32 [256, 256, 1024], P(('dp', 'mod'))
- tokens_grad: float32 [256, 256, 1024], P(('dp', 'mod'))
- condition_grad: float32 [256, 1024], P(('dp', 'mod'))
- modulation_weight_grad: float32 [1024, 6144], P('dp', 'mod')
- modulation_bias_grad: float32 [6, 1024], P('mod', 'dp')
- input_weight_grad: float32 [1024, 3072], P(('dp', 'mod'))
- query_bias_grad: float32 [1024], P(('dp', 'mod'))
- value_bias_grad: float32 [1024], P(('dp', 'mod'))
- output_weight_grad: float32 [1024, 1024], P(('dp', 'mod'))
- output_bias_grad: float32 [1024], P(('dp', 'mod'))
- expand_weight_grad: float32 [1024, 4096], P(('dp', 'mod'))
- expand_bias_grad: float32 [4096], P(('dp', 'mod'))
- contract_weight_grad: float32 [4096, 1024], P(('dp', 'mod'))
- contract_bias_grad: float32 [1024], P(('dp', 'mod'))
Inputs may be any that keep to these rules, and one draw needn't show every extreme that they name: Slots come in aligned groups of 2 held by one device; the images of a group with occupied = 1 are its first 1 to 2 slots, every group has one, and some group has all 2.
All inputs are finite; a program needn't handle non-finite values.
Results may differ from a plain program's by a relative error of at most 0.017.
The roundings to bfloat16 on the way count: a program that leaves them out, or rounds other values in their place, can miss the bound.
Values may be sent and summed in bfloat16 or wider, within the bound.
No kernel may reach another device: no remote copies, remote signals or barrier semaphores. Data moves between devices by JAX's collectives and lax.ppermute only.
A program may use at most 256 MiB of HBM per device.

v0:
```python
import functools

import jax
import jax.numpy as jnp
import numpy as np
from jax import lax
from jax.experimental import pallas as pl
from jax.experimental.pallas import tpu as pltpu
from jax.sharding import Mesh
from jax.sharding import PartitionSpec as P

HEAD_DIM = 64
LANES = 128


def _nt(a, b):
    return lax.dot_general(a, b, (((1,), (1,)), ((), ())), preferred_element_type=jnp.float32)


def _tn(a, b):
    return lax.dot_general(a, b, (((0,), (0,)), ((), ())), preferred_element_type=jnp.float32)


def _probs(q, k, head, factor):
    lane = lax.broadcasted_iota(jnp.int32, (1, LANES), 1)
    mine = (lane // HEAD_DIM) == head
    qh = jnp.where(mine, q, jnp.zeros_like(q))
    scores = _nt(qh, k) * factor
    weights = jnp.exp(scores - jnp.max(scores, axis=-1, keepdims=True))
    return mine, qh, weights / jnp.sum(weights, axis=-1, keepdims=True)


def _fwd_kernel(factor, q_ref, k_ref, v_ref, o_ref):
    def pair(j, carry):
        cols = pl.ds(pl.multiple_of(j * LANES, LANES), LANES)
        q = q_ref[:, cols]
        k = k_ref[:, cols]
        v = v_ref[:, cols]
        out = jnp.zeros((q.shape[0], LANES), jnp.float32)
        for head in range(LANES // HEAD_DIM):
            mine, _, probs = _probs(q, k, head, factor)
            vh = jnp.where(mine, v, jnp.zeros_like(v))
            out = out + jnp.dot(probs.astype(v.dtype), vh, preferred_element_type=jnp.float32)
        o_ref[:, cols] = out.astype(o_ref.dtype)
        return carry

    lax.fori_loop(0, o_ref.shape[1] // LANES, pair, 0, unroll=4)


def _bwd_kernel(factor, q_ref, k_ref, v_ref, d_ref, dq_ref, dk_ref, dv_ref):
    def pair(j, carry):
        cols = pl.ds(pl.multiple_of(j * LANES, LANES), LANES)
        q = q_ref[:, cols]
        k = k_ref[:, cols]
        v = v_ref[:, cols]
        d = d_ref[:, cols]
        dq = jnp.zeros((q.shape[0], LANES), jnp.float32)
        dk = jnp.zeros((q.shape[0], LANES), jnp.float32)
        dv = jnp.zeros((q.shape[0], LANES), jnp.float32)
        for head in range(LANES // HEAD_DIM):
            mine, qh, probs = _probs(q, k, head, factor)
            dh = jnp.where(mine, d, jnp.zeros_like(d))
            kh = jnp.where(mine, k, jnp.zeros_like(k))
            dprobs = _nt(dh, v)
            dv = dv + _tn(probs.astype(d.dtype), dh)
            inner = jnp.sum(dprobs * probs, axis=-1, keepdims=True)
            dscores = (probs * (dprobs - inner)).astype(q.dtype)
            dq = dq + jnp.dot(dscores, kh, preferred_element_type=jnp.float32)
            dk = dk + _tn(dscores, qh)
        dq_ref[:, cols] = (dq * factor).astype(dq_ref.dtype)
        dk_ref[:, cols] = (dk * factor).astype(dk_ref.dtype)
        dv_ref[:, cols] = dv.astype(dv_ref.dtype)
        return carry

    lax.fori_loop(0, dq_ref.shape[1] // LANES, pair, 0, unroll=4)


def _wgrad_kernel(expand_tiles, modb_ref, du_ref, act_ref, dz_ref, out_ref):
    j = pl.program_id(0)

    @pl.when(j < expand_tiles)
    def _():
        out_ref[...] = jnp.dot(
            modb_ref[...], du_ref[...], preferred_element_type=jnp.float32
        ).astype(out_ref.dtype)

    @pl.when(j >= expand_tiles)
    def _():
        out_ref[...] = jnp.dot(
            act_ref[...], dz_ref[...], preferred_element_type=jnp.float32
        ).astype(out_ref.dtype)


def ffn_weight_grads(mod_t, grad_exp, act_t, grad_branch, tile=1024):
    width, tokens = mod_t.shape
    ff = grad_exp.shape[1]
    expand_tiles = ff // tile
    per_part = width // tile
    tiles = expand_tiles + (ff // width) * per_part

    def act_index(j):
        return (jnp.maximum(j - expand_tiles, 0) // per_part, 0)

    def dz_index(j):
        return (0, jnp.maximum(j - expand_tiles, 0) % per_part)

    return pl.pallas_call(
        functools.partial(_wgrad_kernel, expand_tiles),
        out_shape=jax.ShapeDtypeStruct((width, tiles * tile), jnp.bfloat16),
        grid=(tiles,),
        in_specs=[
            pl.BlockSpec((width, tokens), lambda j: (0, 0)),
            pl.BlockSpec((tokens, tile), lambda j: (0, jnp.minimum(j, expand_tiles - 1))),
            pl.BlockSpec((width, tokens), act_index),
            pl.BlockSpec((tokens, tile), dz_index),
        ],
        out_specs=pl.BlockSpec((width, tile), lambda j: (0, j)),
        compiler_params=pltpu.CompilerParams(dimension_semantics=("arbitrary",)),
        cost_estimate=pl.CostEstimate(
            flops=2 * tokens * width * tiles * tile,
            transcendentals=0,
            bytes_accessed=2 * (tokens * (width + 2 * ff + width) + width * tiles * tile),
        ),
    )(mod_t, grad_exp, act_t, grad_branch)

def attention_forward(projected, images):
    tokens, three = projected.shape
    rows, width = tokens // images, three // 3
    pairs = width // LANES
    factor = HEAD_DIM ** (-0.5)

    def part(offset):
        return pl.BlockSpec((rows, width), lambda b: (b, offset))

    flops = 2 * 2 * images * (width // HEAD_DIM) * rows * rows * LANES
    return pl.pallas_call(
        functools.partial(_fwd_kernel, factor),
        out_shape=jax.ShapeDtypeStruct((tokens, width), projected.dtype),
        grid=(images,),
        in_specs=[part(0), part(1), part(2)],
        out_specs=part(0),
        compiler_params=pltpu.CompilerParams(dimension_semantics=("parallel",)),
        cost_estimate=pl.CostEstimate(
            flops=flops, transcendentals=images * (width // HEAD_DIM) * rows * rows,
            bytes_accessed=2 * tokens * (three + width),
        ),
    )(projected, projected, projected)


def attention_backward(projected, grad_attended, images):
    tokens, three = projected.shape
    rows, width = tokens // images, three // 3
    pairs = width // LANES
    factor = HEAD_DIM ** (-0.5)

    def part(offset):
        return pl.BlockSpec((rows, width), lambda b: (b, offset))

    out = jax.ShapeDtypeStruct((tokens, width), projected.dtype)
    flops = 5 * 2 * 2 * images * (width // HEAD_DIM) * rows * rows * LANES
    dq, dk, dv = pl.pallas_call(
        functools.partial(_bwd_kernel, factor),
        out_shape=(out, out, out),
        grid=(images,),
        in_specs=[part(0), part(1), part(2), part(0)],
        out_specs=[part(0)] * 3,
        compiler_params=pltpu.CompilerParams(dimension_semantics=("parallel",)),
        cost_estimate=pl.CostEstimate(
            flops=flops, transcendentals=images * (width // HEAD_DIM) * rows * rows,
            bytes_accessed=2 * tokens * (three + 4 * width),
        ),
    )(projected, projected, projected, grad_attended)
    return jnp.concatenate([dq, dk, dv], axis=1)


EPS = 1e-06
GELU_C = 0.7978845608028654

AXES = ("y", "zh", "x", "c", "zl")
DP = ("y", "zh", "x", "c")
STAGES = ("c", "x", "y", "zh", "zl")
STAGES_B = ("c", "y", "x", "zh", "zl")


def matmul(left, right):
    return jnp.dot(left, right, preferred_element_type=jnp.float32)


def left_trans(left, right):
    return lax.dot_general(
        left, right, (((0,), (0,)), ((), ())), preferred_element_type=jnp.float32
    )


def right_trans(left, right):
    return lax.dot_general(
        left, right, (((1,), (1,)), ((), ())), preferred_element_type=jnp.float32
    )


def normalize(values):
    centre = values - jnp.mean(values, axis=-1, keepdims=True)
    inverse = lax.rsqrt(jnp.mean(centre * centre, axis=-1, keepdims=True) + EPS)
    return (centre * inverse, inverse)


def norm_back(grad, normed, inverse):
    return inverse * (
        grad
        - jnp.mean(grad, axis=-1, keepdims=True)
        - normed * jnp.mean(grad * normed, axis=-1, keepdims=True)
    )


def stage_order(values, sizes, inner, stages=STAGES):
    lead = values.shape[:-1]
    shape = [sizes[a] for a in AXES]
    values = values.reshape(*lead, *shape, inner)
    n = len(lead)
    order = list(range(n)) + [n + AXES.index(a) for a in stages] + [n + len(AXES)]
    return jnp.transpose(values, order).reshape(*lead, -1)


def reduce_stages(packed, stages):
    for a in stages:
        packed = lax.psum_scatter(packed, a, scatter_dimension=0, tiled=True)
    return packed


def reduce_pair(packed, axis):
    half = packed.shape[0] // 2
    index = lax.axis_index(axis)
    keep = lax.dynamic_slice_in_dim(packed, index * half, half, axis=0)
    send = lax.dynamic_slice_in_dim(packed, (1 - index) * half, half, axis=0)
    got = lax.ppermute(send, axis, [(0, 1), (1, 0)])
    return (keep.astype(jnp.float32) + got.astype(jnp.float32)).astype(packed.dtype)


def reduce_rest(packed, axes):
    count = 1
    for a in axes:
        count *= lax.axis_size(a)
    chunks = packed.reshape(count, packed.shape[0] // count, packed.shape[1])
    chunks = lax.all_to_all(chunks, axes, 0, 0, tiled=False)
    return jnp.sum(chunks.astype(jnp.float32), axis=0)


def bias_columns(columns, rows):
    block = jnp.stack(columns, axis=1)
    return jnp.pad(block, ((0, 0), (0, 128 - block.shape[1]))).astype(jnp.bfloat16)


def gather_dp(values):
    count = 1
    for a in DP:
        count *= lax.axis_size(a)
    copies = jnp.broadcast_to(values[None], (count,) + values.shape)
    return lax.all_to_all(copies, DP, 0, 0, tiled=False).reshape(-1, values.shape[1])


def per_device(
    sizes,
    tokens,
    condition,
    occupied,
    modulation_weight,
    modulation_bias,
    input_weight,
    query_bias,
    value_bias,
    output_weight,
    output_bias,
    expand_weight,
    expand_bias,
    contract_weight,
    contract_bias,
    cotangent,
):
    images, rows, width = tokens.shape
    heads = width // HEAD_DIM
    flat = images * rows
    factor = HEAD_DIM ** (-0.5)
    cond_full = condition.astype(jnp.float32)
    sigmoid = jax.nn.sigmoid(cond_full)
    silu_b = (cond_full * sigmoid).astype(jnp.bfloat16)
    swap = [(0, 1), (1, 0)]
    first = lax.axis_index("zl") == 0
    silu_other = lax.ppermute(silu_b, "zl", swap)
    silu_pair = jnp.where(
        first,
        jnp.concatenate([silu_b, silu_other], axis=0),
        jnp.concatenate([silu_other, silu_b], axis=0),
    )
    mod_cols = matmul(silu_pair, modulation_weight) + modulation_bias.reshape(1, -1)
    own_cols = jnp.where(first, mod_cols[:images], mod_cols[images:])
    sent_cols = jnp.where(first, mod_cols[images:], mod_cols[:images])
    other_cols = lax.ppermute(sent_cols, "zl", swap)
    modulation = jnp.where(
        first,
        jnp.concatenate([own_cols, other_cols], axis=1),
        jnp.concatenate([other_cols, own_cols], axis=1),
    ).reshape(images, 6, 1, width)
    shift_a = modulation[:, 0]
    scale_a = modulation[:, 1]
    gate_a = modulation[:, 2]
    shift_b = modulation[:, 3]
    scale_b = modulation[:, 4]
    gate_b = modulation[:, 5]
    inputs = tokens.astype(jnp.float32)
    normed_a, inverse_a = normalize(inputs)
    mod_a = (normed_a * (1.0 + scale_a) + shift_a).astype(jnp.bfloat16).reshape(flat, width)
    qkv_bias = jnp.concatenate([query_bias, jnp.zeros_like(query_bias), value_bias])
    projected = (matmul(mod_a, input_weight) + qkv_bias).astype(jnp.bfloat16)
    attended_b = attention_forward(projected, images)
    branch_a = (matmul(attended_b, output_weight) + output_bias).reshape(images, rows, width)
    middle = inputs + gate_a * branch_a
    normed_b, inverse_b = normalize(middle)
    mod_b = (normed_b * (1.0 + scale_b) + shift_b).astype(jnp.bfloat16).reshape(flat, width)
    expanded = matmul(mod_b, expand_weight) + expand_bias
    tanh_part = jnp.tanh(GELU_C * (expanded + 0.044715 * expanded * expanded * expanded))
    activated_b = (0.5 * expanded * (1.0 + tanh_part)).astype(jnp.bfloat16)
    branch_b = (matmul(activated_b, contract_weight) + contract_bias).reshape(images, rows, width)
    alive = occupied.astype(jnp.float32)[:, None, None]
    layer_out = (middle + gate_b * branch_b) * alive
    grad_out = cotangent.astype(jnp.float32) * alive
    grad_gate_b = jnp.sum(grad_out * branch_b, axis=1)
    grad_branch_b = (grad_out * gate_b).astype(jnp.bfloat16).reshape(flat, width)
    blocks = 1
    for a in AXES:
        blocks *= sizes[a]
    ff = activated_b.shape[1]
    split = ff // width
    act_perm = stage_order(
        activated_b.reshape(flat, blocks, split, width // blocks)
        .transpose(0, 2, 1, 3)
        .reshape(flat, split, width),
        sizes,
        width // blocks,
    )
    contract_bias_grad = stage_order(
        jnp.sum(grad_branch_b.astype(jnp.float32), axis=0), sizes, width // blocks, STAGES_B
    )
    grad_act = right_trans(grad_branch_b, contract_weight)
    slope = 0.5 * (1.0 + tanh_part) + 0.5 * expanded * (1.0 - tanh_part * tanh_part) * GELU_C * (
        1.0 + 3.0 * 0.044715 * expanded * expanded
    )
    grad_exp_b = (grad_act * slope).astype(jnp.bfloat16)
    expand_bias_grad = stage_order(
        jnp.sum(grad_exp_b.astype(jnp.float32), axis=0)
        .reshape(blocks, split, width // blocks)
        .transpose(1, 0, 2)
        .reshape(split, width),
        sizes,
        width // blocks,
        STAGES_B,
    )
    packed_a = ffn_weight_grads(
        stage_order(mod_b, sizes, width // blocks).T, grad_exp_b, act_perm.reshape(flat, -1).T, grad_branch_b
    )
    packed_a, grad_exp_b = lax.optimization_barrier((packed_a, grad_exp_b))
    chain_a = reduce_stages(packed_a, STAGES[:1])
    grad_mod_b = right_trans(grad_exp_b, expand_weight).reshape(images, rows, width)
    grad_shift_b = jnp.sum(grad_mod_b, axis=1)
    grad_scale_b = jnp.sum(grad_mod_b * normed_b, axis=1)
    grad_middle = grad_out + norm_back(grad_mod_b * (1.0 + scale_b), normed_b, inverse_b)
    grad_gate_a = jnp.sum(grad_middle * branch_a, axis=1)
    grad_branch_a = (grad_middle * gate_a).astype(jnp.bfloat16).reshape(flat, width)
    output_grad = left_trans(stage_order(attended_b, sizes, width // blocks, STAGES_B), grad_branch_a).astype(
        jnp.bfloat16
    )
    output_bias_grad = stage_order(
        jnp.sum(grad_branch_a.astype(jnp.float32), axis=0), sizes, width // blocks, STAGES_B
    )
    grad_att_b = right_trans(grad_branch_a, output_weight).astype(jnp.bfloat16)
    chain_a, grad_att_b = lax.optimization_barrier((chain_a, grad_att_b))
    chain_a = reduce_stages(chain_a, STAGES[1:2])
    grad_proj_b = attention_backward(projected, grad_att_b, images)
    input_grad = left_trans(stage_order(mod_a, sizes, width // blocks, STAGES_B), grad_proj_b).astype(
        jnp.bfloat16
    )
    bias_sums = jnp.sum(grad_proj_b.astype(jnp.float32), axis=0)
    query_bias_grad = stage_order(bias_sums[:width], sizes, width // blocks, STAGES_B)
    value_bias_grad = stage_order(bias_sums[2 * width :], sizes, width // blocks, STAGES_B)
    chain_b = reduce_pair(
        jnp.concatenate(
            [
                input_grad,
                output_grad,
                bias_columns(
                [query_bias_grad, value_bias_grad, output_bias_grad, contract_bias_grad]
                + [expand_bias_grad[q] for q in range(split)],
                width,
            ),
            ],
            axis=1,
        ),
        STAGES_B[0],
    )
    chain_a, chain_b = lax.optimization_barrier((chain_a, chain_b))
    chain_b = reduce_stages(chain_b, STAGES_B[1:2])
    grad_mod_a = right_trans(grad_proj_b, input_weight).reshape(images, rows, width)
    grad_shift_a = jnp.sum(grad_mod_a, axis=1)
    grad_scale_a = jnp.sum(grad_mod_a * normed_a, axis=1)
    tokens_grad = grad_middle + norm_back(grad_mod_a * (1.0 + scale_a), normed_a, inverse_a)
    modulation_terms = jnp.stack(
        [grad_shift_a, grad_scale_a, grad_gate_a, grad_shift_b, grad_scale_b, grad_gate_b], axis=1
    ).reshape(images, 6 * width)
    modulation_own = modulation_terms.astype(jnp.bfloat16)
    half = modulation_own.shape[1] // 2
    keep_cols = jnp.where(first, modulation_own[:, :half], modulation_own[:, half:])
    give_cols = jnp.where(first, modulation_own[:, half:], modulation_own[:, :half])
    got_cols = lax.ppermute(give_cols, "zl", swap)
    modulation_cols = jnp.where(
        first,
        jnp.concatenate([keep_cols, got_cols], axis=0),
        jnp.concatenate([got_cols, keep_cols], axis=0),
    )
    silu_terms = right_trans(modulation_cols, modulation_weight)
    pair_index = lax.axis_index("zl")
    own_rows = lax.dynamic_slice_in_dim(silu_terms, pair_index * images, images, axis=0)
    other_rows = lax.dynamic_slice_in_dim(silu_terms, (1 - pair_index) * images, images, axis=0)
    silu_sums = own_rows + lax.ppermute(other_rows, "zl", [(0, 1), (1, 0)])
    condition_grad = silu_sums * sigmoid * (1.0 + cond_full * (1.0 - sigmoid))
    dp_count = lax.axis_size(DP)
    cores = lax.axis_size("c")
    peers = dp_count // cores
    row_block = width // dp_count
    cols = modulation_cols.shape[1]
    silu_parts = silu_pair.reshape(-1, peers, cores * row_block).transpose(1, 0, 2)
    silu_parts = jnp.pad(silu_parts, ((0, 0), (0, 0), (0, 128 - cores * row_block)))
    payload = jnp.concatenate(
        [jnp.broadcast_to(modulation_cols[None], (peers,) + modulation_cols.shape), silu_parts], axis=2
    )
    near = lax.all_to_all(payload, ("y", "zh", "x"), 0, 0, tiled=False)
    far = lax.ppermute(near, "c", [(0, 1), (1, 0)])
    factors = jnp.concatenate([near, far], axis=0)
    mod_all = factors[:, :, :cols].reshape(-1, cols)
    silu_rows = lax.dynamic_slice_in_dim(
        factors[:, :, cols : cols + cores * row_block], lax.axis_index("c") * row_block, row_block, axis=2
    ).reshape(-1, row_block)
    dp_index = lax.axis_index(DP)
    modulation_weight_grad = left_trans(silu_rows, mod_all)
    bias_all = jnp.sum(mod_all.astype(jnp.float32), axis=0).reshape(-1, width)
    modulation_bias_grad = lax.dynamic_slice_in_dim(bias_all, dp_index * row_block, row_block, axis=1)
    chain_a = reduce_rest(chain_a, STAGES[2:])
    chain_b, mod_all = lax.optimization_barrier((chain_b, mod_all))
    chain_b = reduce_rest(chain_b, STAGES_B[2:])
    three = input_weight.shape[1]
    fw = expand_weight.shape[1]
    input_weight_grad = chain_b[:, :three]
    output_weight_grad = chain_b[:, three : three + width]
    qb_grad = chain_b[:, three + width]
    vb_grad = chain_b[:, three + width + 1]
    ob_grad = chain_b[:, three + width + 2]
    expand_weight_grad = chain_a[:, :fw]
    contract_weight_grad = chain_a[:, fw : fw + split * width].reshape(-1, split, width)
    contract_weight_grad = contract_weight_grad.transpose(1, 0, 2).reshape(-1, width)
    cb_grad = chain_b[:, three + width + 3]
    eb_grad = chain_b[:, three + width + 4 : three + width + 4 + split].T.reshape(-1)
    summed = (
        input_weight_grad,
        qb_grad,
        vb_grad,
        output_weight_grad,
        ob_grad,
        expand_weight_grad,
        eb_grad,
        contract_weight_grad,
        cb_grad,
    )
    return (
        layer_out,
        tokens_grad,
        condition_grad,
        modulation_weight_grad,
        modulation_bias_grad,
        *summed,
    )


def solution(mesh):
    dp_size, mod_size = mesh.devices.shape
    rest = dp_size // 4
    side = int(round(rest ** 0.5))
    shape = (side, 2, rest // side, 2, mod_size)
    sizes = dict(zip(AXES, shape))
    physical = Mesh(np.asarray(mesh.devices).reshape(shape), AXES)
    ALL = AXES
    placed = (
        P(ALL, None, None),
        P(ALL, None),
        P(ALL),
        P(None, "zl"),
        P("zl", None),
        P(),
        P(),
        P(),
        P(),
        P(),
        P(),
        P(),
        P(),
        P(),
        P(ALL, None, None),
    )
    return jax.shard_map(
        functools.partial(per_device, sizes),
        mesh=physical,
        in_specs=placed,
        out_specs=(
            P(ALL, None, None),
            P(ALL, None, None),
            P(ALL, None),
            P(DP, "zl"),
            P("zl", DP),
            P(ALL, None),
            P(ALL),
            P(ALL),
            P(ALL, None),
            P(ALL),
            P(ALL, None),
            P(ALL),
            P(ALL, None),
            P(ALL),
        ),
        check_vma=False,
    )
```

profile of v0, /device:TPU:0, one launch (start us, length us, event | category | flops | bytes accessed | tf_op | source)
XLA Modules:
  0.0 352.2 jit_solution(13171169401730253141)
XLA Ops:
  8.1 2.1 collective-permute-start
  13.4 3.8 %convolution_add_fusion = f32[4,3072]{1,0:T(4,128)S(1)} fusion(bf16[1024,3072]{1,0:T(8,128)(2,1)} %param.18, f32[3072]{0:T(1024)S(1)} %add.177, bf16[2,1024]{1,0:T(2,128)(2,1)S(1)} %collective-permute-done, bf16[2,1024]{1,0:T(2,128)(2,1)S(1)} %fusion.34, pred[]{:T(512)S(6)} %eq.3), kind=kOutput, calls=%fused_computation.18 | convolution fusion | flops 25214976 | bytes 6361089 | tf_op jit(solution)/shard_map/dot_general | solution.py:186
  17.7 3.4 collective-permute-done.1
  22.7 7.5 %add_convert_fusion.1.q_ref.k_ref.v_ref = bf16[512,3072]{1,0:T(8,128)(2,1)} fusion(bf16[512,1024]{1,0:T(8,128)(2,1)S(1)} %bitcast.126, bf16[1024,3072]{1,0:T(8,128)(2,1)} %param.20, f32[3072]{0:T(1024)S(1)} %pad_maximum_fusion), kind=kOutput, calls=%fused_computation.14 | convolution fusion | flops 3224371200 | bytes 10498048 | tf_op jit(solution)/shard_map/dot_general | solution.py:186
  30.3 9.1 %shard_map.254 = bf16[512,1024]{1,0:T(8,128)(2,1)} custom-call(bf16[512,3072]{1,0:T(8,128)(2,1)} %add_convert_fusion.1.q_ref.k_ref.v_ref, bf16[512,3072]{1,0:T(8,128)(2,1)} %add_convert_fusion.1.q_ref.k_ref.v_ref, bf16[512,3072]{1,0:T(8,128)(2,1)} %add_convert_fusion.1.q_ref.k_ref.v_ref), custom_call_target="tpu_custom_call" | custom-call | flops 1073741824 | bytes 4194304 | tf_op jit(solution)/shard_map/pallas_call | solution.py:136
  39.3 2.5 convolution_add_fusion.1
  45.9 3.7 %copy.62 = bf16[2,256,1024]{1,0,2:T(2,128)(2,1)} copy(bf16[2,256,1024]{2,1,0:T(8,128)(2,1)} %add_convert_fusion.2) | data formatting | bytes 2097152 | tf_op jit(solution)/shard_map/convert_element_type | solution.py:318
  49.6 2.5 reshape_reshape.15
  52.1 2.4 copy.63
  54.5 12.7 %multiply_convert_fusion = (bf16[512,4096]{1,0:T(8,128)(2,1)}, f32[512,4096]{1,0:T(8,128)}) fusion(f32[4096]{0:T(1024)S(1)} %copy-done.22, bf16[512,1024]{1,0:T(8,128)(2,1)S(1)} %bitcast.128, bf16[1024,4096]{1,0:T(8,128)(2,1)} %param.25), kind=kOutput, calls=%fused_computation.13 | convolution fusion | flops 4315938816 | bytes 22036480 | tf_op jit(solution)/shard_map/dot_general | solution.py:186
  67.2 6.5 %copy.64 = bf16[512,4096]{0,1:T(8,128)(2,1)} copy(bf16[512,4096]{1,0:T(8,128)(2,1)} %get-tuple-element.73) | data formatting | bytes 8388608 | tf_op jit(solution)/shard_map/convert_element_type | solution.py:321
  73.6 5.1 %copy.66 = bf16[512,4,2,4,4,2,2,8]{0,7,6,5,4,3,2,1:T(8,128)(2,1)} copy(bf16[512,4,2,4,4,2,2,8]{0,7,1,6,2,3,5,4:T(8,128)(2,1)} %bitcast.123) | data formatting | bytes 8388608 | tf_op jit(solution)/shard_map/transpose | solution.py:221
  80.1 23.0 %fusion.53 = (bf16[4096]{0:T(1024)(128)(2,1)S(1)}, bf16[512,4096]{1,0:T(8,128)(2,1)}) fusion(f32[512,4096]{1,0:T(8,128)S(1)} %copy-done.26, f32[4096]{0:T(1024)S(1)} %copy-done.22, bf16[512,1024]{1,0:T(8,128)(2,1)S(1)} %bitcast.136, bf16[4096,1024]{1,0:T(8,128)(2,1)} %param.27), kind=kOutput, calls=%fused_computation.136 | convolution fusion | flops 4339003392 | bytes 22044672 | tf_op jit(solution)/shard_map/dot_general | solution.py:196
  103.1 16.0 %shard_map.255 = bf16[1024,8192]{1,0:T(8,128)(2,1)} custom-call(bf16[1024,512]{1,0:T(8,128)(2,1)} %bitcast.135, bf16[512,4096]{1,0:T(8,128)(2,1)} %get-tuple-element.23.du_ref, bf16[4096,512]{1,0:T(8,128)(2,1)} %bitcast.125, bf16[512,1024]{1,0:T(8,128)(2,1)} %bitcast.137), custom_call_target="tpu_custom_call" | custom-call | flops 8589934592 | bytes 27262976 | tf_op jit(solution)/shard_map/pallas_call | solution.py:107
  119.2 10.5 %fusion.24 = (f32[512]{0:T(512)S(1)}, f32[512,1024]{1,0:T(8,128)}) fusion(f32[2,1024]{1,0:T(2,128)S(1)} %get-tuple-element.82, bf16[512,4096]{1,0:T(8,128)(2,1)} %get-tuple-element.23.du_ref, bf16[1024,4096]{1,0:T(8,128)(2,1)} %param.25), kind=kOutput, calls=%fused_computation.42 | convolution fusion | flops 4296015360 | bytes 14690304 | tf_op jit(solution)/shard_map/dot_general | solution.py:196
  129.7 9.4 %convolution_add_fusion.2 = f32[512,1024]{1,0:T(8,128)S(1)} fusion(bf16[512,4096]{1,0:T(8,128)(2,1)} %get-tuple-element.73, bf16[4096,1024]{1,0:T(8,128)(2,1)} %param.27, f32[1024]{0:T(1024)S(1)} %copy-done.24), kind=kOutput, calls=%fused_computation.61 | convolution fusion | flops 4295491584 | bytes 14684160 | tf_op jit(solution)/shard_map/dot_general | solution.py:186
  139.2 2.7 fusion.25
  141.9 2.4 fusion.46
  145.3 2.3 convolution_convert_fusion.2.d_ref
  147.6 2.6 reduce-scatter.4.cloned.1.call-done
  150.3 4.1 %copy.74 = bf16[2,256,1024]{1,0,2:T(2,128)(2,1)} copy(bf16[2,256,1024]{2,1,0:T(8,128)(2,1)} %copy-done.11) | data formatting | bytes 2097152 | tf_op jit(solution)/shard_map/convert_element_type | solution.py:311
  154.4 2.3 copy.76
  156.7 2.5 reshape_reshape.18
  159.2 2.3 copy.75
  161.8 2.4 copy.77
  165.2 4.2 %convolution_convert_fusion.1 = bf16[1024,1024]{1,0:T(8,128)(2,1)} fusion(bf16[512,1024]{0,1:T(8,128)(2,1)} %bitcast.134, bf16[512,1024]{1,0:T(8,128)(2,1)} %bitcast.139), kind=kOutput, calls=%fused_computation.57 | convolution fusion | flops 1074790400 | bytes 4194304 | tf_op jit(solution)/shard_map/dot_general | solution.py:190
  169.4 16.8 %shard_map.256 = (bf16[512,1024]{1,0:T(8,128)(2,1)}, bf16[512,1024]{1,0:T(8,128)(2,1)}, bf16[512,1024]{1,0:T(8,128)(2,1)}) custom-call(bf16[512,3072]{1,0:T(8,128)(2,1)} %add_convert_fusion.1.q_ref.k_ref.v_ref, bf16[512,3072]{1,0:T(8,128)(2,1)} %add_convert_fusion.1.q_ref.k_ref.v_ref, bf16[512,3072]{1,0:T(8,128)(2,1)} %add_convert_fusion.1.q_ref.k_ref.v_ref, ...), custom_call_target="tpu_custom_call" | custom-call | flops 5368709120 | bytes 7340032 | tf_op jit(solution)/shard_map/pallas_call | solution.py:161
  186.2 2.5 constant_dynamic-update-slice_fusion.2
  190.9 2.6 reduce.5
  194.2 6.0 %convolution_convert_fusion = bf16[1024,3072]{1,0:T(8,128)(2,1)S(1)} fusion(bf16[512,1024]{0,1:T(8,128)(2,1)} %bitcast.133, bf16[512,3072]{1,0:T(8,128)(2,1)} %constant_dynamic-update-slice_fusion), kind=kOutput, calls=%fused_computation.15 | convolution fusion | flops 3224371200 | bytes 10485760 | tf_op jit(solution)/shard_map/dot_general | solution.py:190
  200.9 2.5 constant_dynamic-slice_fusion
  203.4 2.1 copy-done.4
  206.1 7.3 %collective-permute-done.5 = bf16[512,4224]{1,0:T(8,128)(2,1)} collective-permute-done((bf16[512,4224]{1,0:T(8,128)(2,1)}, bf16[512,4224]{1,0:T(8,128)(2,1)}, u32[]{:S(2)}, u32[]{:S(2)}) %collective-permute-start.5) | collective-permute-done | bytes 4325408 | tf_op jit(solution)/shard_map/ppermute | solution.py:235
  213.4 6.6 %add_convert_fusion = bf16[512,4224]{1,0:T(8,128)(2,1)} fusion(bf16[512,4224]{1,0:T(8,128)(2,1)} %collective-permute-done.5, bf16[1024,4224]{1,0:T(8,128)(2,1)} %copy-done.4, s32[]{:T(128)S(6)} %select_n.97), kind=kLoop, calls=%fused_computation.5 | loop fusion | flops 8650752 | bytes 12976132 | tf_op jit(solution)/shard_map/convert_element_type | solution.py:236
  220.0 14.7 %reduce-scatter.6.cloned.1.call-done = bf16[128,8192]{1,0:T(8,128)(2,1)} async-done(((bf16[512,8192]{1,0:T(8,128)(2,1)}), bf16[128,8192]{1,0:T(8,128)(2,1)}) %reduce-scatter.6.cloned.1.call-update) | async-done | bytes 2097168 | tf_op jit(solution)/shard_map/reduce_scatter | solution.py:226
  235.0 8.5 %fusion.23 = (f32[512]{0:T(512)S(1)}, f32[512,1024]{1,0:T(8,128)}) fusion(f32[2,1024]{1,0:T(2,128)S(1)} %get-tuple-element.85, bf16[512,3072]{1,0:T(8,128)(2,1)} %constant_dynamic-update-slice_fusion, bf16[1024,3072]{1,0:T(8,128)(2,1)} %param.20), kind=kOutput, calls=%fused_computation.39 | convolution fusion | flops 3222273536 | bytes 11544576 | tf_op jit(solution)/shard_map/dot_general | solution.py:196
  243.5 3.3 fusion.21
  247.8 3.9 %multiply_reduce_fusion.1 = (bf16[2,1024]{1,0:T(2,128)(2,1)S(1)}, f32[2,256,1024]{2,1,0:T(8,128)}) fusion(f32[2,256,1024]{2,1,0:T(8,128)} %get-tuple-element.46, f32[512,1024]{1,0:T(8,128)S(1)} %copy-done.10, f32[2,256]{1,0:T(2,128)S(1)} %broadcast_multiply_fusion.2, f32[2,256]{1,0:T(2,128)S(1)} %broadcast_multiply_fusion.5, ...), kind=kLoop, calls=%fused_computation.47 | loop fusion | flops 5765120 | bytes 9457664 | tf_op jit(solution)/shard_map/reduce_sum | solution.py:366
  253.4 2.1 collective-permute-done.2
  256.2 23.6 %all_to_all.15 = bf16[32,4,3200]{2,1,0:T(4,128)(2,1)S(1)} all-to-all(bf16[32,4,3200]{2,1,0:T(4,128)(2,1)S(1)} %fusion.28), channel_id=1, replica_groups=mesh['y'=4,'zh'=2,'x'=4,'c'=2,'zl'=2] {'y','zh','x'}, dimensions={0} | all-to-all | bytes 1638400 | tf_op jit(solution)/shard_map/all_to_all | solution.py:434
  279.8 4.4 %all-to-all-start.2 = ((bf16[16,8,8192]{2,1,0:T(8,128)(2,1)}), bf16[16,8,8192]{2,1,0:T(8,128)(2,1)}, u32[]{:S(2)}, u32[]{:S(2)}) async-start(bf16[16,8,8192]{2,1,0:T(8,128)(2,1)} %bitcast.131), calls=%async_computation.5 | async-start | bytes 4194304 | tf_op jit(solution)/shard_map/all_to_all | solution.py:244
  285.6 4.5 %fusion.54 = f32[4,1024]{1,0:T(4,128)S(1)} fusion(bf16[4,3072]{1,0:T(4,128)(2,1)S(1)} %maximum_select_fusion.2, bf16[1024,3072]{1,0:T(8,128)(2,1)} %param.18), kind=kOutput, calls=%fused_computation.137 | convolution fusion | flops 25165824 | bytes 6332416 | tf_op jit(solution)/shard_map/dot_general | solution.py:196
  291.9 1.9 collective-permute-done.3
  298.7 2.5 convolution_bitcast_fusion
  301.8 18.2 %all-to-all-done.2 = bf16[16,8,8192]{2,1,0:T(8,128)(2,1)} async-done(((bf16[16,8,8192]{2,1,0:T(8,128)(2,1)}), bf16[16,8,8192]{2,1,0:T(8,128)(2,1)}, u32[]{:S(2)}, u32[]{:S(2)}) %all-to-all-start.2) | async-done | bytes 2097184 | tf_op jit(solution)/shard_map/all_to_all | solution.py:244
  320.0 5.3 %all-to-all-start.1 = ((bf16[16,8,4224]{2,1,0:T(8,128)(2,1)}), bf16[16,8,4224]{2,1,0:T(8,128)(2,1)S(1)}, u32[]{:S(2)}, u32[]{:S(2)}) async-start(bf16[16,8,4224]{2,1,0:T(8,128)(2,1)} %bitcast.132), calls=%async_computation.4 | async-start | bytes 2162688 | tf_op jit(solution)/shard_map/all_to_all | solution.py:244
  325.4 1.9 convert_reduce_fusion
  328.0 14.6 %all-to-all-done.1 = bf16[16,8,4224]{2,1,0:T(8,128)(2,1)S(1)} async-done(((bf16[16,8,4224]{2,1,0:T(8,128)(2,1)}), bf16[16,8,4224]{2,1,0:T(8,128)(2,1)S(1)}, u32[]{:S(2)}, u32[]{:S(2)}) %all-to-all-start.1) | async-done | bytes 1081376 | tf_op jit(solution)/shard_map/all_to_all | solution.py:244
  (157 shorter events, 33.7 us)
Async XLA Ops:
  7.2 32.1 %copy-start = (bf16[1024,1024]{1,0:T(8,128)(2,1)S(1)}, bf16[1024,1024]{1,0:T(8,128)(2,1)}, u32[]{:S(2)}) copy-start(bf16[1024,1024]{1,0:T(8,128)(2,1)} %param.23) | copy-start | bytes 6291460
  7.2 6.1 %copy-start.18 = (f32[3,1024]{1,0:T(4,128)S(1)}, f32[3,1024]{1,0:T(4,128)}, u32[]{:S(2)}) copy-start(f32[3,1024]{1,0:T(4,128)} %param.19) | copy-start | bytes 36868
  7.2 143.0 %reduce-scatter.4.cloned.1.call-start = ((), (), s32[]{:S(2)}) async-start(), calls=%async_computation.6 | async-start | bytes 25165824 | tf_op jit(solution)/shard_map/reduce_scatter | solution.py:226
  8.1 5.3 %collective-permute-start = (bf16[2,1024]{1,0:T(2,128)(2,1)S(1)}, bf16[2,1024]{1,0:T(2,128)(2,1)S(1)}, u32[]{:S(2)}, u32[]{:S(2)}) collective-permute-start(bf16[2,1024]{1,0:T(2,128)(2,1)S(1)} %fusion.34), channel_id=1, source_target_pairs={{0,1},{1,0},{2,3},{3,2},{4,5},{5,4},{6,7},{7,6},{8,9},{9,8},{10,11... | collective-permute-start | bytes 12296 | tf_op jit(solution)/shard_map/ppermute | solution.py:288
  13.3 4.3 %copy-start.20 = (f32[1024]{0:T(1024)S(1)}, f32[1024]{0:T(1024)}, u32[]{:S(2)}) copy-start(f32[1024]{0:T(1024)} %param.22) | copy-start | bytes 12292
  13.3 4.3 %copy-start.21 = (f32[1024]{0:T(1024)S(1)}, f32[1024]{0:T(1024)}, u32[]{:S(2)}) copy-start(f32[1024]{0:T(1024)} %param.21) | copy-start | bytes 12292
  13.3 4.3 %copy-start.25 = (s32[2]{0:T(128)S(1)}, s32[2]{0:T(128)}, u32[]{:S(2)}) copy-start(s32[2]{0:T(128)} %param.17) | copy-start | bytes 28
  13.3 7.9 %copy-start.3 = (bf16[2,256,1024]{2,1,0:T(8,128)(2,1)S(1)}, bf16[2,256,1024]{2,1,0:T(8,128)(2,1)}, u32[]{:S(2)}) copy-start(bf16[2,256,1024]{2,1,0:T(8,128)(2,1)} %param.15) | copy-start | bytes 3145732
  17.2 3.9 %collective-permute-start.1 = (f32[2,3072]{1,0:T(2,128)S(1)}, f32[2,3072]{1,0:T(2,128)S(1)}, u32[]{:S(2)}, u32[]{:S(2)}) collective-permute-start(f32[2,3072]{1,0:T(2,128)S(1)} %get-tuple-element.67), channel_id=1, source_target_pairs={{0,1},{1,0},{2,3},{3,2},{4,5},{5,4},{6,7},{7,6},{8,9},{9,8},{10,11... | collective-permute-start | bytes 73736 | tf_op jit(solution)/shard_map/ppermute | solution.py:297
  21.7 1.0 copy-start.11
  30.3 9.1 %copy-start.23 = (f32[1024]{0:T(1024)S(1)}, f32[1024]{0:T(1024)}, u32[]{:S(2)}) copy-start(f32[1024]{0:T(1024)} %param.24) | copy-start | bytes 12292
  41.8 1.4 copy-start.9
  43.2 1.3 copy-start.1
  49.6 4.9 %copy-start.22 = (f32[4096]{0:T(1024)S(1)}, f32[4096]{0:T(1024)}, u32[]{:S(2)}) copy-start(f32[4096]{0:T(1024)} %param.26) | copy-start | bytes 49156
  52.1 2.4 copy-start.12
  73.6 5.1 %copy-start.7 = (bf16[2,256,1024]{2,1,0:T(8,128)(2,1)S(1)}, bf16[2,256,1024]{2,1,0:T(8,128)(2,1)}, u32[]{:S(2)}) copy-start(bf16[2,256,1024]{2,1,0:T(8,128)(2,1)} %param.29) | copy-start | bytes 3145732
  73.6 6.5 %copy-start.26 = (f32[512,4096]{1,0:T(8,128)S(1)}, f32[512,4096]{1,0:T(8,128)}, u32[]{:S(2)}) copy-start(f32[512,4096]{1,0:T(8,128)} %get-tuple-element.74) | copy-start | bytes 25165828
  79.2 23.9 %copy-start.14 = (bf16[2,256,1024]{2,1,0:T(8,128)(2,1)}, bf16[2,256,1024]{2,1,0:T(8,128)(2,1)S(1)}, u32[]{:S(2)}) copy-start(bf16[2,256,1024]{2,1,0:T(8,128)(2,1)S(1)} %get-tuple-element.43) | copy-start | bytes 3145732
  119.1 10.6 %copy-start.24 = (f32[1024]{0:T(1024)S(1)}, f32[1024]{0:T(1024)}, u32[]{:S(2)}) copy-start(f32[1024]{0:T(1024)} %param.28) | copy-start | bytes 12292
  119.1 115.6 %reduce-scatter.6.cloned.1.call-start = ((), (), s32[]{:S(2)}) async-start(), calls=%async_computation.7 | async-start | bytes 10485760 | tf_op jit(solution)/shard_map/reduce_scatter | solution.py:226
  129.7 9.5 %copy-start.2 = (f32[2,256,1024]{2,1,0:T(8,128)S(1)}, f32[2,256,1024]{2,1,0:T(8,128)}, u32[]{:S(2)}) copy-start(f32[2,256,1024]{2,1,0:T(8,128)} %copy-done.1) | copy-start | bytes 6291460
  129.7 9.5 %copy-start.5 = (f32[512,1024]{1,0:T(8,128)S(1)}, f32[512,1024]{1,0:T(8,128)}, u32[]{:S(2)}) copy-start(f32[512,1024]{1,0:T(8,128)} %get-tuple-element.76) | copy-start | bytes 6291460
  129.7 9.5 %copy-start.8 = (bf16[2,256,1024]{2,1,0:T(8,128)(2,1)S(1)}, bf16[2,256,1024]{2,1,0:T(8,128)(2,1)}, u32[]{:S(2)}) copy-start(bf16[2,256,1024]{2,1,0:T(8,128)(2,1)} %param.29) | copy-start | bytes 3145732
  144.3 1.0 copy-start.17
  150.2 151.5 %reduce-scatter.8.cloned.1.call-start = ((), (), s32[]{:S(2)}) async-start(), calls=%async_computation.8 | async-start | bytes 5406720 | tf_op jit(solution)/shard_map/reduce_scatter | solution.py:226
  186.2 2.5 copy-start.16
  186.2 3.6 %copy-start.15 = (bf16[512,1024]{1,0:T(8,128)(2,1)S(1)}, bf16[512,1024]{1,0:T(8,128)(2,1)}, u32[]{:S(2)}) copy-start(bf16[512,1024]{1,0:T(8,128)(2,1)} %get-tuple-element.28) | copy-start | bytes 3145732
  194.2 6.0 %copy-start.13 = (bf16[1024,1024]{1,0:T(8,128)(2,1)S(1)}, bf16[1024,1024]{1,0:T(8,128)(2,1)}, u32[]{:S(2)}) copy-start(bf16[1024,1024]{1,0:T(8,128)(2,1)} %convolution_convert_fusion.1) | copy-start | bytes 6291460
  200.9 4.6 %copy-start.4 = (bf16[1024,4224]{1,0:T(8,128)(2,1)}, bf16[1024,4224]{1,0:T(8,128)(2,1)S(1)}, u32[]{:S(2)}) copy-start(bf16[1024,4224]{1,0:T(8,128)(2,1)S(1)} %fusion.1) | copy-start | bytes 25952260
  205.5 7.9 %collective-permute-start.5 = (bf16[512,4224]{1,0:T(8,128)(2,1)}, bf16[512,4224]{1,0:T(8,128)(2,1)}, u32[]{:S(2)}, u32[]{:S(2)}) collective-permute-start(bf16[512,4224]{1,0:T(8,128)(2,1)} %constant_dynamic-slice_fusion), channel_id=1, source_target_pairs={{0,2},{2,0},{1,3},{3,1},{4,6},{6,4},{5,7},{7,5},{8,10},{10,8},{9,1... | collective-permute-start | bytes 12976136 | tf_op jit(solution)/shard_map/ppermute | solution.py:235
  243.5 3.4 copy-start.6
  243.5 4.3 %copy-start.10 = (f32[512,1024]{1,0:T(8,128)S(1)}, f32[512,1024]{1,0:T(8,128)}, u32[]{:S(2)}) copy-start(f32[512,1024]{1,0:T(8,128)} %copy-done.9) | copy-start | bytes 6291460
  251.8 3.8 %collective-permute-start.2 = (bf16[2,3072]{1,0:T(2,128)(2,1)S(1)}, bf16[2,3072]{1,0:T(2,128)(2,1)S(1)}, u32[]{:S(2)}, u32[]{:S(2)}) collective-permute-start(bf16[2,3072]{1,0:T(2,128)(2,1)S(1)} %get-tuple-element.69), channel_id=1, source_target_pairs={{0,1},{1,0},{2,3},{3,2},{4,5},{5,4},{6,7},{7,6},{8,9},{9,8},{10,11... | collective-permute-start | bytes 36872 | tf_op jit(solution)/shard_map/ppermute | solution.py:412
  279.8 40.2 %all-to-all-start.2 = ((bf16[16,8,8192]{2,1,0:T(8,128)(2,1)}), bf16[16,8,8192]{2,1,0:T(8,128)(2,1)}, u32[]{:S(2)}, u32[]{:S(2)}) async-start(bf16[16,8,8192]{2,1,0:T(8,128)(2,1)} %bitcast.131), calls=%async_computation.5 | async-start | bytes 4194304 | tf_op jit(solution)/shard_map/all_to_all | solution.py:244
  285.6 8.9 %collective-permute-start.4 = (bf16[32,4,3200]{2,0,1:T(8,128)(2,1)}, bf16[32,4,3200]{2,0,1:T(8,128)(2,1)S(1)}, u32[]{:S(2)}, u32[]{:S(2)}) collective-permute-start(bf16[32,4,3200]{2,0,1:T(8,128)(2,1)} %get-tuple-element.52), channel_id=1, source_target_pairs={{0,2},{2,0},{1,3},{3,1},{4,6},{6,4},{5,7},{7,5},{8,10},{10,8},{9,1... | collective-permute-start | bytes 2457608 | tf_op jit(solution)/shard_map/ppermute | solution.py:435
  285.6 8.3 %copy-start.19 = (bf16[2,1024]{1,0:T(2,128)(2,1)S(1)}, bf16[2,1024]{1,0:T(2,128)(2,1)}, u32[]{:S(2)}) copy-start(bf16[2,1024]{1,0:T(2,128)(2,1)} %param.16) | copy-start | bytes 12292
  290.1 3.8 %collective-permute-start.3 = (f32[2,1024]{1,0:T(2,128)S(1)}, f32[2,1024]{1,0:T(2,128)S(1)}, u32[]{:S(2)}, u32[]{:S(2)}) collective-permute-start(f32[2,1024]{1,0:T(2,128)S(1)} %constant_dynamic-slice_fusion.2), channel_id=1, source_target_pairs={{0,1},{1,0},{2,3},{3,2},{4,5},{5,4},{6,7},{7,6},{8,9},{9,8},{10,11... | collective-permute-start | bytes 24584 | tf_op jit(solution)/shard_map/ppermute | solution.py:422
  320.0 22.6 %all-to-all-start.1 = ((bf16[16,8,4224]{2,1,0:T(8,128)(2,1)}), bf16[16,8,4224]{2,1,0:T(8,128)(2,1)S(1)}, u32[]{:S(2)}, u32[]{:S(2)}) async-start(bf16[16,8,4224]{2,1,0:T(8,128)(2,1)} %bitcast.132), calls=%async_computation.4 | async-start | bytes 2162688 | tf_op jit(solution)/shard_map/all_to_all | solution.py:244
Sparse Core Ops, SparseCore 0:
  119.2 30.9 reduce-scatter.3
  152.8 81.8 reduce-scatter.5
  237.3 64.4 reduce-scatter.7
where the time goes:
time: 357 us; the launch traced here: 352 us
  matrix products  97.4 us (27%)
  waiting for transfers between devices  65.6 us (18%)
  local copies, waits for them, and re-layouts  58.7 us (16%)
  Pallas kernels  41.8 us (12%)
  other arithmetic  34.2 us (10%)
  blocking collectives  23.6 us (7%)
  starting transfers between devices  16.3 us (5%)
  between operations  14.5 us (4%)
    dot_general x5, matrix products, right_trans(): lax.dot_general(left, right, (((1,), (1,)), ((), ())), preferred_element_...  48.8 us
    dot_general x5, matrix products, matmul(): return jnp.dot(left, right, preferred_element_type=jnp.float32)  35.9 us
    all_to_all x2, waiting for transfers between devices, reduce_rest(): chunks = lax.all_to_all(chunks, axes, 0, 0, tiled=False)  32.8 us
    all_to_all x1, blocking collectives, per_device(): near = lax.all_to_all(payload, ('y', 'zh', 'x'), 0, 0, tiled=False)  23.6 us
    reduce_scatter x3, waiting for transfers between devices, reduce_stages(): packed = lax.psum_scatter(packed, a, scatter_dimension=0, tiled=True)  17.9 us
    pallas_call x1, Pallas kernels, attention_backward(): pl.pallas_call(functools.partial(_bwd_kernel, factor), out_shape=(out, ou...  16.8 us
    pallas_call x1, Pallas kernels, ffn_weight_grads(): pl.pallas_call(functools.partial(_wgrad_kernel, expand_tiles), out_shape=...  16 us
    dot_general x3, matrix products, left_trans(): lax.dot_general(left, right, (((0,), (0,)), ((), ())), preferred_element_...  12.7 us
  transfers between devices with their start and end apart: 11, of which 9 were waited for; matrix products, arithmetic and copies ran while one was open for 30% of the time, Pallas kernels for 5%

commit v1 on v0

--- a/solution.py
+++ b/solution.py
@@ -179,7 +179,7 @@
 AXES = ("y", "zh", "x", "c", "zl")
 DP = ("y", "zh", "x", "c")
 STAGES = ("c", "x", "y", "zh", "zl")
-STAGES_B = ("c", "y", "x", "zh", "zl")
+STAGES_B = STAGES
 
 
 def matmul(left, right):
@@ -442,9 +442,10 @@
     modulation_weight_grad = left_trans(silu_rows, mod_all)
     bias_all = jnp.sum(mod_all.astype(jnp.float32), axis=0).reshape(-1, width)
     modulation_bias_grad = lax.dynamic_slice_in_dim(bias_all, dp_index * row_block, row_block, axis=1)
-    chain_a = reduce_rest(chain_a, STAGES[2:])
     chain_b, mod_all = lax.optimization_barrier((chain_b, mod_all))
-    chain_b = reduce_rest(chain_b, STAGES_B[2:])
+    rest = reduce_rest(jnp.concatenate([chain_a, chain_b], axis=1), STAGES[2:])
+    chain_a = rest[:, : chain_a.shape[1]]
+    chain_b = rest[:, chain_a.shape[1] :]
     three = input_weight.shape[1]
     fw = expand_weight.shape[1]
     input_weight_grad = chain_b[:, :three]

time: 357 us -> 370 us (1.036)
  the two profiles are of different devices: /device:TPU:0 before, /device:TPU:24 now
where the time goes in v1:
time: 370 us; the launch traced here: 364 us
  matrix products  97.4 us (26%)
  waiting for transfers between devices  90.8 us (25%)
  local copies, waits for them, and re-layouts  58.8 us (16%)
  Pallas kernels  41.8 us (11%)
  other arithmetic  39.1 us (11%)
  starting transfers between devices  21.7 us (6%)
  between operations  14.5 us (4%)
    dot_general x5, matrix products, right_trans(): lax.dot_general(left, right, (((1,), (1,)), ((), ())), preferred_element_...  48.8 us
    reduce_scatter x3, waiting for transfers between devices, reduce_stages(): packed = lax.psum_scatter(packed, a, scatter_dimension=0, tiled=True)  45.5 us
    dot_general x5, matrix products, matmul(): return jnp.dot(left, right, preferred_element_type=jnp.float32)  35.9 us
    ppermute x1, waiting for transfers between devices, per_device(): silu_sums = own_rows + lax.ppermute(other_rows, 'zl', [(0, 1), (1, 0)])  32.3 us
    pallas_call x1, Pallas kernels, attention_backward(): pl.pallas_call(functools.partial(_bwd_kernel, factor), out_shape=(out, ou...  16.8 us
    pallas_call x1, Pallas kernels, ffn_weight_grads(): pl.pallas_call(functools.partial(_wgrad_kernel, expand_tiles), out_shape=...  16 us
    dot_general x3, matrix products, left_trans(): lax.dot_general(left, right, (((0,), (0,)), ((), ())), preferred_element_...  12.7 us
    transpose x8, local copies, waits for them, and re-layouts, stage_order(): return jnp.transpose(values, order).reshape(*lead, -1)  12.3 us
  transfers between devices with their start and end apart: 11, of which 7 were waited for; matrix products, arithmetic and copies ran while one was open for 30% of the time, Pallas kernels for 5%

profile of v1, /device:TPU:24, one launch (start us, length us, event | category | flops | bytes accessed | tf_op | source)
XLA Modules:
  0.0 364.1 jit_solution(17272072490138301339)
XLA Ops:
  8.1 2.0 collective-permute-start
  13.3 3.8 %convolution_add_fusion = f32[4,3072]{1,0:T(4,128)S(1)} fusion(bf16[1024,3072]{1,0:T(8,128)(2,1)} %param.18, f32[3072]{0:T(1024)S(1)} %add.177, bf16[2,1024]{1,0:T(2,128)(2,1)S(1)} %collective-permute-done, bf16[2,1024]{1,0:T(2,128)(2,1)S(1)} %fusion.34, pred[]{:T(512)S(6)} %eq.3), kind=kOutput, calls=%fused_computation.18 | convolution fusion | flops 25214976 | bytes 6361089 | tf_op jit(solution)/shard_map/dot_general | solution.py:186
  17.6 3.4 collective-permute-done.1
  22.6 7.5 %add_convert_fusion.1.q_ref.k_ref.v_ref = bf16[512,3072]{1,0:T(8,128)(2,1)} fusion(bf16[512,1024]{1,0:T(8,128)(2,1)S(1)} %bitcast.126, bf16[1024,3072]{1,0:T(8,128)(2,1)} %param.20, f32[3072]{0:T(1024)S(1)} %pad_maximum_fusion), kind=kOutput, calls=%fused_computation.15 | convolution fusion | flops 3224371200 | bytes 10498048 | tf_op jit(solution)/shard_map/dot_general | solution.py:186
  30.2 9.0 %shard_map.254 = bf16[512,1024]{1,0:T(8,128)(2,1)} custom-call(bf16[512,3072]{1,0:T(8,128)(2,1)} %add_convert_fusion.1.q_ref.k_ref.v_ref, bf16[512,3072]{1,0:T(8,128)(2,1)} %add_convert_fusion.1.q_ref.k_ref.v_ref, bf16[512,3072]{1,0:T(8,128)(2,1)} %add_convert_fusion.1.q_ref.k_ref.v_ref), custom_call_target="tpu_custom_call" | custom-call | flops 1073741824 | bytes 4194304 | tf_op jit(solution)/shard_map/pallas_call | solution.py:136
  39.2 2.5 convolution_add_fusion.1
  45.8 3.7 %copy.62 = bf16[2,256,1024]{1,0,2:T(2,128)(2,1)} copy(bf16[2,256,1024]{2,1,0:T(8,128)(2,1)} %add_convert_fusion.2) | data formatting | bytes 2097152 | tf_op jit(solution)/shard_map/convert_element_type | solution.py:318
  49.5 2.5 reshape_reshape.15
  52.0 2.4 copy.63
  54.4 12.7 %multiply_convert_fusion = (bf16[512,4096]{1,0:T(8,128)(2,1)}, f32[512,4096]{1,0:T(8,128)}) fusion(f32[4096]{0:T(1024)S(1)} %copy-done.22, bf16[512,1024]{1,0:T(8,128)(2,1)S(1)} %bitcast.128, bf16[1024,4096]{1,0:T(8,128)(2,1)} %param.25), kind=kOutput, calls=%fused_computation.13 | convolution fusion | flops 4315938816 | bytes 22036480 | tf_op jit(solution)/shard_map/dot_general | solution.py:186
  67.1 6.5 %copy.64 = bf16[512,4096]{0,1:T(8,128)(2,1)} copy(bf16[512,4096]{1,0:T(8,128)(2,1)} %get-tuple-element.73) | data formatting | bytes 8388608 | tf_op jit(solution)/shard_map/convert_element_type | solution.py:321
  73.5 5.1 %copy.66 = bf16[512,4,2,4,4,2,2,8]{0,7,6,5,4,3,2,1:T(8,128)(2,1)} copy(bf16[512,4,2,4,4,2,2,8]{0,7,1,6,2,3,5,4:T(8,128)(2,1)} %bitcast.123) | data formatting | bytes 8388608 | tf_op jit(solution)/shard_map/transpose | solution.py:221
  80.0 23.0 %fusion.53 = (bf16[4096]{0:T(1024)(128)(2,1)S(1)}, bf16[512,4096]{1,0:T(8,128)(2,1)}) fusion(f32[512,4096]{1,0:T(8,128)S(1)} %copy-done.26, f32[4096]{0:T(1024)S(1)} %copy-done.22, bf16[512,1024]{1,0:T(8,128)(2,1)S(1)} %bitcast.134, bf16[4096,1024]{1,0:T(8,128)(2,1)} %param.27), kind=kOutput, calls=%fused_computation.136 | convolution fusion | flops 4339003392 | bytes 22044672 | tf_op jit(solution)/shard_map/dot_general | solution.py:196
  103.0 16.0 %shard_map.255 = bf16[1024,8192]{1,0:T(8,128)(2,1)} custom-call(bf16[1024,512]{1,0:T(8,128)(2,1)} %bitcast.133, bf16[512,4096]{1,0:T(8,128)(2,1)} %get-tuple-element.23.du_ref, bf16[4096,512]{1,0:T(8,128)(2,1)} %bitcast.125, bf16[512,1024]{1,0:T(8,128)(2,1)} %bitcast.135), custom_call_target="tpu_custom_call" | custom-call | flops 8589934592 | bytes 27262976 | tf_op jit(solution)/shard_map/pallas_call | solution.py:107
  119.1 10.5 %fusion.24 = (f32[512]{0:T(512)S(1)}, f32[512,1024]{1,0:T(8,128)}) fusion(f32[2,1024]{1,0:T(2,128)S(1)} %get-tuple-element.82, bf16[512,4096]{1,0:T(8,128)(2,1)} %get-tuple-element.23.du_ref, bf16[1024,4096]{1,0:T(8,128)(2,1)} %param.25), kind=kOutput, calls=%fused_computation.42 | convolution fusion | flops 4296015360 | bytes 14690304 | tf_op jit(solution)/shard_map/dot_general | solution.py:196
  129.6 9.4 %convolution_add_fusion.2 = f32[512,1024]{1,0:T(8,128)S(1)} fusion(bf16[512,4096]{1,0:T(8,128)(2,1)} %get-tuple-element.73, bf16[4096,1024]{1,0:T(8,128)(2,1)} %param.27, f32[1024]{0:T(1024)S(1)} %copy-done.24), kind=kOutput, calls=%fused_computation.61 | convolution fusion | flops 4295491584 | bytes 14684160 | tf_op jit(solution)/shard_map/dot_general | solution.py:186
  139.1 2.7 fusion.25
  141.8 2.4 fusion.46
  145.2 2.3 convolution_convert_fusion.2.d_ref
  147.5 2.5 reduce-scatter.4.cloned.1.call-done
  150.0 4.1 %copy.74 = bf16[2,256,1024]{1,0,2:T(2,128)(2,1)} copy(bf16[2,256,1024]{2,1,0:T(8,128)(2,1)} %copy-done.11) | data formatting | bytes 2097152 | tf_op jit(solution)/shard_map/convert_element_type | solution.py:311
  154.1 2.3 copy.76
  156.5 2.5 reshape_reshape.18
  159.0 2.3 copy.75
  161.5 2.4 copy.77
  165.0 4.2 %convolution_convert_fusion.1 = bf16[1024,1024]{1,0:T(8,128)(2,1)} fusion(bf16[512,1024]{0,1:T(8,128)(2,1)} %bitcast.132, bf16[512,1024]{1,0:T(8,128)(2,1)} %bitcast.137), kind=kOutput, calls=%fused_computation.57 | convolution fusion | flops 1074790400 | bytes 4194304 | tf_op jit(solution)/shard_map/dot_general | solution.py:190
  169.2 16.8 %shard_map.256 = (bf16[512,1024]{1,0:T(8,128)(2,1)}, bf16[512,1024]{1,0:T(8,128)(2,1)}, bf16[512,1024]{1,0:T(8,128)(2,1)}) custom-call(bf16[512,3072]{1,0:T(8,128)(2,1)} %add_convert_fusion.1.q_ref.k_ref.v_ref, bf16[512,3072]{1,0:T(8,128)(2,1)} %add_convert_fusion.1.q_ref.k_ref.v_ref, bf16[512,3072]{1,0:T(8,128)(2,1)} %add_convert_fusion.1.q_ref.k_ref.v_ref, ...), custom_call_target="tpu_custom_call" | custom-call | flops 5368709120 | bytes 7340032 | tf_op jit(solution)/shard_map/pallas_call | solution.py:161
  186.0 2.5 constant_dynamic-update-slice_fusion.2
  190.7 2.6 reduce.5
  194.0 6.0 %convolution_convert_fusion = bf16[1024,3072]{1,0:T(8,128)(2,1)S(1)} fusion(bf16[512,1024]{0,1:T(8,128)(2,1)} %bitcast.131, bf16[512,3072]{1,0:T(8,128)(2,1)} %constant_dynamic-update-slice_fusion), kind=kOutput, calls=%fused_computation.16 | convolution fusion | flops 3224371200 | bytes 10485760 | tf_op jit(solution)/shard_map/dot_general | solution.py:190
  200.7 2.5 constant_dynamic-slice_fusion
  203.2 2.1 copy-done.4
  205.7 7.4 %collective-permute-done.5 = bf16[512,4224]{1,0:T(8,128)(2,1)} collective-permute-done((bf16[512,4224]{1,0:T(8,128)(2,1)}, bf16[512,4224]{1,0:T(8,128)(2,1)}, u32[]{:S(2)}, u32[]{:S(2)}) %collective-permute-start.5) | collective-permute-done | bytes 4325408 | tf_op jit(solution)/shard_map/ppermute | solution.py:235
  213.1 6.6 %add_convert_fusion = bf16[512,4224]{1,0:T(8,128)(2,1)} fusion(bf16[512,4224]{1,0:T(8,128)(2,1)} %collective-permute-done.5, bf16[1024,4224]{1,0:T(8,128)(2,1)} %copy-done.4, s32[]{:T(128)S(6)} %select_n.97), kind=kLoop, calls=%fused_computation.5 | loop fusion | flops 8650752 | bytes 12976132 | tf_op jit(solution)/shard_map/convert_element_type | solution.py:236
  219.8 14.6 %reduce-scatter.6.cloned.1.call-done = bf16[128,8192]{1,0:T(8,128)(2,1)} async-done(((bf16[512,8192]{1,0:T(8,128)(2,1)}), bf16[128,8192]{1,0:T(8,128)(2,1)}) %reduce-scatter.6.cloned.1.call-update) | async-done | bytes 2097168 | tf_op jit(solution)/shard_map/reduce_scatter | solution.py:226
  234.6 8.5 %fusion.23 = (f32[512]{0:T(512)S(1)}, f32[512,1024]{1,0:T(8,128)}) fusion(f32[2,1024]{1,0:T(2,128)S(1)} %get-tuple-element.85, bf16[512,3072]{1,0:T(8,128)(2,1)} %constant_dynamic-update-slice_fusion, bf16[1024,3072]{1,0:T(8,128)(2,1)} %param.20), kind=kOutput, calls=%fused_computation.39 | convolution fusion | flops 3222273536 | bytes 11544576 | tf_op jit(solution)/shard_map/dot_general | solution.py:196
  243.1 3.2 fusion.21
  247.4 3.9 %multiply_reduce_fusion.1 = (bf16[2,1024]{1,0:T(2,128)(2,1)S(1)}, f32[2,256,1024]{2,1,0:T(8,128)}) fusion(f32[2,256,1024]{2,1,0:T(8,128)} %get-tuple-element.46, f32[512,1024]{1,0:T(8,128)S(1)} %copy-done.10, f32[2,256]{1,0:T(2,128)S(1)} %broadcast_multiply_fusion.2, f32[2,256]{1,0:T(2,128)S(1)} %broadcast_multiply_fusion.5, ...), kind=kLoop, calls=%fused_computation.47 | loop fusion | flops 5765120 | bytes 9457664 | tf_op jit(solution)/shard_map/reduce_sum | solution.py:366
  253.1 2.1 collective-permute-done.2
  256.7 8.2 %all-to-all-start = ((bf16[32,4,3200]{2,1,0:T(4,128)(2,1)}), bf16[32,4,3200]{2,1,0:T(4,128)(2,1)S(1)}, u32[]{:S(2)}, u32[]{:S(2)}) async-start(bf16[32,4,3200]{2,1,0:T(4,128)(2,1)} %fusion.28), calls=%async_computation.1 | async-start | bytes 1638400 | tf_op jit(solution)/shard_map/all_to_all | solution.py:434
  264.9 28.4 %reduce-scatter.8.cloned.1.call-done = bf16[128,4224]{1,0:T(8,128)(2,1)} async-done(((bf16[512,4224]{1,0:T(8,128)(2,1)}), bf16[128,4224]{1,0:T(8,128)(2,1)}) %reduce-scatter.8.cloned.1.call-update) | async-done | bytes 1081360 | tf_op jit(solution)/shard_map/reduce_scatter | solution.py:226
  293.3 3.8 %maximum_bitcast_fusion = bf16[16,8,12416]{2,1,0:T(8,128)(2,1)} fusion(bf16[128,4224]{1,0:T(8,128)(2,1)} %reduce-scatter.8.cloned.1.call-done, bf16[128,8192]{1,0:T(8,128)(2,1)} %reduce-scatter.6.cloned.1.call-done), kind=kLoop, calls=%fused_computation.19 | loop fusion | flops 6356992 | bytes 6356992 | tf_op jit(solution)/shard_map/reshape | solution.py:243
  297.1 7.4 %all-to-all-start.1 = ((bf16[16,8,12416]{2,1,0:T(8,128)(2,1)}), bf16[16,8,12416]{2,1,0:T(8,128)(2,1)}, u32[]{:S(2)}, u32[]{:S(2)}) async-start(bf16[16,8,12416]{2,1,0:T(8,128)(2,1)} %maximum_bitcast_fusion), calls=%async_computation.4 | async-start | bytes 6356992 | tf_op jit(solution)/shard_map/all_to_all | solution.py:244
  305.8 4.5 %fusion.54 = f32[4,1024]{1,0:T(4,128)S(1)} fusion(bf16[4,3072]{1,0:T(4,128)(2,1)S(1)} %maximum_select_fusion.2, bf16[1024,3072]{1,0:T(8,128)(2,1)} %param.18), kind=kOutput, calls=%fused_computation.137 | convolution fusion | flops 25165824 | bytes 6332416 | tf_op jit(solution)/shard_map/dot_general | solution.py:196
  311.9 32.3 %collective-permute-done.3 = f32[2,1024]{1,0:T(2,128)S(1)} collective-permute-done((f32[2,1024]{1,0:T(2,128)S(1)}, f32[2,1024]{1,0:T(2,128)S(1)}, u32[]{:S(2)}, u32[]{:S(2)}) %collective-permute-start.3) | collective-permute-done | bytes 8224 | tf_op jit(solution)/shard_map/ppermute | solution.py:422
  346.7 1.7 convert_reduce_fusion.1
  349.0 2.5 convolution_bitcast_fusion
  351.5 2.4 convert_reduce_fusion
  (156 shorter events, 31.8 us)
Async XLA Ops:
  7.2 32.0 %copy-start = (bf16[1024,1024]{1,0:T(8,128)(2,1)S(1)}, bf16[1024,1024]{1,0:T(8,128)(2,1)}, u32[]{:S(2)}) copy-start(bf16[1024,1024]{1,0:T(8,128)(2,1)} %param.23) | copy-start | bytes 6291460
  7.2 6.0 %copy-start.18 = (f32[3,1024]{1,0:T(4,128)S(1)}, f32[3,1024]{1,0:T(4,128)}, u32[]{:S(2)}) copy-start(f32[3,1024]{1,0:T(4,128)} %param.19) | copy-start | bytes 36868
  7.2 142.8 %reduce-scatter.4.cloned.1.call-start = ((), (), s32[]{:S(2)}) async-start(), calls=%async_computation.5 | async-start | bytes 25165824 | tf_op jit(solution)/shard_map/reduce_scatter | solution.py:226
  8.1 5.2 %collective-permute-start = (bf16[2,1024]{1,0:T(2,128)(2,1)S(1)}, bf16[2,1024]{1,0:T(2,128)(2,1)S(1)}, u32[]{:S(2)}, u32[]{:S(2)}) collective-permute-start(bf16[2,1024]{1,0:T(2,128)(2,1)S(1)} %fusion.34), channel_id=1, source_target_pairs={{0,1},{1,0},{2,3},{3,2},{4,5},{5,4},{6,7},{7,6},{8,9},{9,8},{10,11... | collective-permute-start | bytes 12296 | tf_op jit(solution)/shard_map/ppermute | solution.py:288
  13.2 4.3 %copy-start.20 = (f32[1024]{0:T(1024)S(1)}, f32[1024]{0:T(1024)}, u32[]{:S(2)}) copy-start(f32[1024]{0:T(1024)} %param.22) | copy-start | bytes 12292
  13.2 4.3 %copy-start.21 = (f32[1024]{0:T(1024)S(1)}, f32[1024]{0:T(1024)}, u32[]{:S(2)}) copy-start(f32[1024]{0:T(1024)} %param.21) | copy-start | bytes 12292
  13.2 4.3 %copy-start.25 = (s32[2]{0:T(128)S(1)}, s32[2]{0:T(128)}, u32[]{:S(2)}) copy-start(s32[2]{0:T(128)} %param.17) | copy-start | bytes 28
  13.3 7.9 %copy-start.3 = (bf16[2,256,1024]{2,1,0:T(8,128)(2,1)S(1)}, bf16[2,256,1024]{2,1,0:T(8,128)(2,1)}, u32[]{:S(2)}) copy-start(bf16[2,256,1024]{2,1,0:T(8,128)(2,1)} %param.15) | copy-start | bytes 3145732
  17.1 3.9 %collective-permute-start.1 = (f32[2,3072]{1,0:T(2,128)S(1)}, f32[2,3072]{1,0:T(2,128)S(1)}, u32[]{:S(2)}, u32[]{:S(2)}) collective-permute-start(f32[2,3072]{1,0:T(2,128)S(1)} %get-tuple-element.67), channel_id=1, source_target_pairs={{0,1},{1,0},{2,3},{3,2},{4,5},{5,4},{6,7},{7,6},{8,9},{9,8},{10,11... | collective-permute-start | bytes 73736 | tf_op jit(solution)/shard_map/ppermute | solution.py:297
  21.6 1.0 copy-start.11
  30.2 9.1 %copy-start.23 = (f32[1024]{0:T(1024)S(1)}, f32[1024]{0:T(1024)}, u32[]{:S(2)}) copy-start(f32[1024]{0:T(1024)} %param.24) | copy-start | bytes 12292
  41.7 1.4 copy-start.9
  43.1 1.3 copy-start.1
  49.5 4.9 %copy-start.22 = (f32[4096]{0:T(1024)S(1)}, f32[4096]{0:T(1024)}, u32[]{:S(2)}) copy-start(f32[4096]{0:T(1024)} %param.26) | copy-start | bytes 49156
  52.0 2.4 copy-start.12
  73.5 5.1 %copy-start.7 = (bf16[2,256,1024]{2,1,0:T(8,128)(2,1)S(1)}, bf16[2,256,1024]{2,1,0:T(8,128)(2,1)}, u32[]{:S(2)}) copy-start(bf16[2,256,1024]{2,1,0:T(8,128)(2,1)} %param.29) | copy-start | bytes 3145732
  73.5 6.5 %copy-start.26 = (f32[512,4096]{1,0:T(8,128)S(1)}, f32[512,4096]{1,0:T(8,128)}, u32[]{:S(2)}) copy-start(f32[512,4096]{1,0:T(8,128)} %get-tuple-element.74) | copy-start | bytes 25165828
  79.1 23.9 %copy-start.14 = (bf16[2,256,1024]{2,1,0:T(8,128)(2,1)}, bf16[2,256,1024]{2,1,0:T(8,128)(2,1)S(1)}, u32[]{:S(2)}) copy-start(bf16[2,256,1024]{2,1,0:T(8,128)(2,1)S(1)} %get-tuple-element.43) | copy-start | bytes 3145732
  119.0 10.6 %copy-start.24 = (f32[1024]{0:T(1024)S(1)}, f32[1024]{0:T(1024)}, u32[]{:S(2)}) copy-start(f32[1024]{0:T(1024)} %param.28) | copy-start | bytes 12292
  119.0 115.3 %reduce-scatter.6.cloned.1.call-start = ((), (), s32[]{:S(2)}) async-start(), calls=%async_computation.6 | async-start | bytes 10485760 | tf_op jit(solution)/shard_map/reduce_scatter | solution.py:226
  129.6 9.5 %copy-start.2 = (f32[2,256,1024]{2,1,0:T(8,128)S(1)}, f32[2,256,1024]{2,1,0:T(8,128)}, u32[]{:S(2)}) copy-start(f32[2,256,1024]{2,1,0:T(8,128)} %copy-done.1) | copy-start | bytes 6291460
  129.6 9.5 %copy-start.5 = (f32[512,1024]{1,0:T(8,128)S(1)}, f32[512,1024]{1,0:T(8,128)}, u32[]{:S(2)}) copy-start(f32[512,1024]{1,0:T(8,128)} %get-tuple-element.76) | copy-start | bytes 6291460
  129.6 9.5 %copy-start.8 = (bf16[2,256,1024]{2,1,0:T(8,128)(2,1)S(1)}, bf16[2,256,1024]{2,1,0:T(8,128)(2,1)}, u32[]{:S(2)}) copy-start(bf16[2,256,1024]{2,1,0:T(8,128)(2,1)} %param.29) | copy-start | bytes 3145732
  144.3 1.0 copy-start.17
  150.0 143.3 %reduce-scatter.8.cloned.1.call-start = ((), (), s32[]{:S(2)}) async-start(), calls=%async_computation.7 | async-start | bytes 5406720 | tf_op jit(solution)/shard_map/reduce_scatter | solution.py:226
  186.0 2.5 copy-start.16
  186.0 3.6 copy-start.15
  194.0 6.1 %copy-start.13 = (bf16[1024,1024]{1,0:T(8,128)(2,1)S(1)}, bf16[1024,1024]{1,0:T(8,128)(2,1)}, u32[]{:S(2)}) copy-start(bf16[1024,1024]{1,0:T(8,128)(2,1)} %convolution_convert_fusion.1) | copy-start | bytes 6291460
  200.7 4.6 %copy-start.4 = (bf16[1024,4224]{1,0:T(8,128)(2,1)}, bf16[1024,4224]{1,0:T(8,128)(2,1)S(1)}, u32[]{:S(2)}) copy-start(bf16[1024,4224]{1,0:T(8,128)(2,1)S(1)} %fusion.1) | copy-start | bytes 25952260
  205.3 7.8 %collective-permute-start.5 = (bf16[512,4224]{1,0:T(8,128)(2,1)}, bf16[512,4224]{1,0:T(8,128)(2,1)}, u32[]{:S(2)}, u32[]{:S(2)}) collective-permute-start(bf16[512,4224]{1,0:T(8,128)(2,1)} %constant_dynamic-slice_fusion), channel_id=1, source_target_pairs={{0,2},{2,0},{1,3},{3,1},{4,6},{6,4},{5,7},{7,5},{8,10},{10,8},{9,1... | collective-permute-start | bytes 12976136 | tf_op jit(solution)/shard_map/ppermute | solution.py:235
  243.1 3.3 copy-start.6
  243.1 4.3 %copy-start.10 = (f32[512,1024]{1,0:T(8,128)S(1)}, f32[512,1024]{1,0:T(8,128)}, u32[]{:S(2)}) copy-start(f32[512,1024]{1,0:T(8,128)} %copy-done.9) | copy-start | bytes 6291460
  251.4 3.8 %collective-permute-start.2 = (bf16[2,3072]{1,0:T(2,128)(2,1)S(1)}, bf16[2,3072]{1,0:T(2,128)(2,1)S(1)}, u32[]{:S(2)}, u32[]{:S(2)}) collective-permute-start(bf16[2,3072]{1,0:T(2,128)(2,1)S(1)} %get-tuple-element.69), channel_id=1, source_target_pairs={{0,1},{1,0},{2,3},{3,2},{4,5},{5,4},{6,7},{7,6},{8,9},{9,8},{10,11... | collective-permute-start | bytes 36872 | tf_op jit(solution)/shard_map/ppermute | solution.py:412
  256.7 40.4 %all-to-all-start = ((bf16[32,4,3200]{2,1,0:T(4,128)(2,1)}), bf16[32,4,3200]{2,1,0:T(4,128)(2,1)S(1)}, u32[]{:S(2)}, u32[]{:S(2)}) async-start(bf16[32,4,3200]{2,1,0:T(4,128)(2,1)} %fusion.28), calls=%async_computation.1 | async-start | bytes 1638400 | tf_op jit(solution)/shard_map/all_to_all | solution.py:434
  297.1 54.4 %all-to-all-start.1 = ((bf16[16,8,12416]{2,1,0:T(8,128)(2,1)}), bf16[16,8,12416]{2,1,0:T(8,128)(2,1)}, u32[]{:S(2)}, u32[]{:S(2)}) async-start(bf16[16,8,12416]{2,1,0:T(8,128)(2,1)} %maximum_bitcast_fusion), calls=%async_computation.4 | async-start | bytes 6356992 | tf_op jit(solution)/shard_map/all_to_all | solution.py:244
  305.8 39.1 %collective-permute-start.4 = (bf16[32,4,3200]{2,0,1:T(8,128)(2,1)}, bf16[32,4,3200]{2,0,1:T(8,128)(2,1)S(1)}, u32[]{:S(2)}, u32[]{:S(2)}) collective-permute-start(bf16[32,4,3200]{2,0,1:T(8,128)(2,1)} %get-tuple-element.52), channel_id=1, source_target_pairs={{0,2},{2,0},{1,3},{3,1},{4,6},{6,4},{5,7},{7,5},{8,10},{10,8},{9,1... | collective-permute-start | bytes 2457608 | tf_op jit(solution)/shard_map/ppermute | solution.py:435
  305.8 38.4 %copy-start.19 = (bf16[2,1024]{1,0:T(2,128)(2,1)S(1)}, bf16[2,1024]{1,0:T(2,128)(2,1)}, u32[]{:S(2)}) copy-start(bf16[2,1024]{1,0:T(2,128)(2,1)} %param.16) | copy-start | bytes 12292
  310.4 33.9 %collective-permute-start.3 = (f32[2,1024]{1,0:T(2,128)S(1)}, f32[2,1024]{1,0:T(2,128)S(1)}, u32[]{:S(2)}, u32[]{:S(2)}) collective-permute-start(f32[2,1024]{1,0:T(2,128)S(1)} %constant_dynamic-slice_fusion.2), channel_id=1, source_target_pairs={{0,1},{1,0},{2,3},{3,2},{4,5},{5,4},{6,7},{7,6},{8,9},{9,8},{10,11... | collective-permute-start | bytes 24584 | tf_op jit(solution)/shard_map/ppermute | solution.py:422
Sparse Core Ops, SparseCore 0:
  119.1 30.7 reduce-scatter.3
  152.6 81.7 reduce-scatter.5
  236.9 56.3 reduce-scatter.7
